TPU v7x, 32 devices: a whole 2x2x4 slice. The times are simulated.
32 devices in a mesh: aux: 16 (over z, y, core), occ: 2 (over x).
Axes of the slice: x: 2, y: 2, z: 4, core: 2. Of those that a mesh axis runs over, the one named last changes fastest.
Arguments:
- factors: bfloat16 [4, 8192, 768], P('occ', 'aux'), may hold values from -0.875 to 0.875
- occ_energy: bfloat16 [4], P('occ'), may hold values from -2 to -0.29882812
- virt_energy: float32 [768], replicated, may hold values from 0.2 to 3
- pairs: int32 [2, 2], P('occ'), may hold values from 0 to 3, as said below
Outputs:
- density: bfloat16 [2, 2, 8192, 768], P('occ', None, 'aux')
Inputs may be any that keep to these rules, and one draw needn't show every extreme that they name: Group g's first orbital pairs[g, 0] is one of the 2 orbitals held at index g of occ; the slab distances (pairs[g, 1] // 2 - g) modulo 2 are all different over the groups.
All inputs are finite; a program needn't handle non-finite values.
Results may differ from a plain program's by a relative error of at most 0.0048.
Values may be sent and summed in bfloat16 or wider, within the bound.
A program may use at most 64 MiB of HBM per device.

v0:
```python
import jax
import jax.numpy as jnp
from jax import lax
from jax.sharding import PartitionSpec as P


def on_device(factors, occ_energy, virt_energy, pairs):
    slab_rows = factors.shape[0]
    occ_index = lax.axis_index("occ")
    first_orbital = pairs[0, 0]
    second_orbital = pairs[0, 1]
    local_first = first_orbital - occ_index * slab_rows
    first_rows = lax.dynamic_index_in_dim(factors, local_first, 0, keepdims=False)
    first_energy = lax.dynamic_index_in_dim(occ_energy, local_first, 0, keepdims=False).astype(
        jnp.float32
    )
    listed = lax.all_gather(pairs, "occ", axis=0, tiled=True)
    wanted = listed[:, 1]
    is_owner = wanted // slab_rows == occ_index
    position = jnp.clip(wanted - occ_index * slab_rows, 0, slab_rows - 1)
    owned_rows = jnp.where(
        is_owner[:, None, None], jnp.take(factors, position, axis=0), jnp.zeros((), jnp.bfloat16)
    )
    owned_energy = jnp.where(
        is_owner, jnp.take(occ_energy, position, axis=0), jnp.zeros((), jnp.bfloat16)
    )
    got_rows, got_energy = (
        lax.all_to_all(owned_rows, "occ", split_axis=0, concat_axis=0, tiled=True),
        lax.all_to_all(owned_energy, "occ", split_axis=0, concat_axis=0, tiled=True),
    )
    source = second_orbital // slab_rows
    second_rows = lax.dynamic_index_in_dim(got_rows, source, 0, keepdims=False)
    second_energy = lax.dynamic_index_in_dim(got_energy, source, 0, keepdims=False)
    pair_energy = first_energy + second_energy.astype(jnp.float32)
    partial_sum = lax.dot_general(
        first_rows, second_rows, (((0,), (0,)), ((), ())), preferred_element_type=jnp.float32
    )
    integrals = lax.psum(partial_sum, "aux")
    denominator = pair_energy - virt_energy[:, None] - virt_energy[None, :]
    amplitudes = ((2.0 * integrals - integrals.T) / denominator).astype(jnp.bfloat16)
    first_density = lax.dot_general(
        second_rows, amplitudes, (((1,), (1,)), ((), ())), preferred_element_type=jnp.float32
    )
    second_density = jnp.dot(first_rows, amplitudes, preferred_element_type=jnp.float32)
    return jnp.stack([first_density, second_density]).astype(jnp.bfloat16)[None]


def solution(mesh):
    in_specs = (P("occ", "aux", None), P("occ"), P(), P("occ", None))
    out_specs = P("occ", None, "aux", None)
    return jax.shard_map(
        on_device, mesh=mesh, in_specs=in_specs, out_specs=out_specs, check_vma=False
    )
```

profile of v0, /device:TPU:1, one launch (start us, length us, event | category | flops | bytes accessed | tf_op | source)
XLA Modules:
  0.0 152.8 jit_solution(5633323666162542834)
XLA Ops:
  6.5 0.0 copy-start
  6.5 4.0 %all-gather = s32[2,1,2]{2,1,0:T(1,128)S(1)} all-gather(s32[1,1,2]{2,1,0:T(1,128)} %bitcast.46), channel_id=1, replica_groups=mesh['aux'=16,'occ'=2] {'occ'}, dimensions={0}, use_global_device_ids=true | all-gather | bytes 24 | tf_op jit(solution)/shard_map/all_gather | solution.py:17
  10.5 0.2 slice_reduce_fusion
  10.7 0.2 and_reduce_fusion
  10.9 0.1 reduce.2
  11.0 0.0 copy-done
  11.0 0.6 gather_fusion
  11.7 1.4 select_select_fusion
  13.1 0.0 copy-start.3
  13.1 3.8 %all-to-all-start = ((bf16[2,512,768]{2,1,0:T(8,128)(2,1)}), bf16[2,512,768]{2,1,0:T(8,128)(2,1)S(1)}, u32[]{:S(2)}, u32[]{:S(2)}) async-start(bf16[2,512,768]{2,1,0:T(8,128)(2,1)} %select_select_fusion), calls=%async_computation | async-start | bytes 3145728 | tf_op jit(solution)/shard_map/all_to_all | solution.py:28
  16.9 0.0 all-reduce.2.cloned.1.call-start
  16.9 0.0 copy-done.3
  16.9 0.6 fusion.17
  20.7 13.9 %all-to-all-done = bf16[2,512,768]{2,1,0:T(8,128)(2,1)S(1)} async-done(((bf16[2,512,768]{2,1,0:T(8,128)(2,1)}), bf16[2,512,768]{2,1,0:T(8,128)(2,1)S(1)}, u32[]{:S(2)}, u32[]{:S(2)}) %all-to-all-start) | async-done | bytes 1572896 | tf_op jit(solution)/shard_map/all_to_all | solution.py:28
  34.6 2.2 %fusion.5 = f32[768,768]{1,0:T(8,128)} fusion(bf16[2,512,768]{2,1,0:T(8,128)(2,1)S(1)} %copy-done, s32[]{:T(128)S(6)} %select_n.76, bf16[2,512,768]{2,1,0:T(8,128)(2,1)S(1)} %all-to-all-done, s32[]{:T(128)S(6)} %select_n.75), kind=kOutput, calls=%fused_computation.12 | convolution fusion | flops 603979776 | bytes 3932168 | tf_op jit(solution)/shard_map/dot_general | solution.py:35
  36.8 0.0 copy-start.1
  36.8 0.0 copy-start.2
  36.8 0.0 all-reduce.2.cloned.1.call-update
  36.9 0.6 copy-done.1
  37.5 0.6 gather_fusion.1
  38.2 0.7 copy.8
  38.8 3.2 %all-to-all-start.1 = ((bf16[2,1,1]{2,1,0:T(2,128)(2,1)}), bf16[2,1,1]{2,1,0:T(2,128)(2,1)S(1)}, u32[]{:S(2)}, u32[]{:S(2)}) async-start(bf16[2,1,1]{2,1,0:T(2,128)(2,1)} %copy.8), calls=%async_computation.1 | async-start | bytes 2048 | tf_op jit(solution)/shard_map/all_to_all | solution.py:29
  42.0 0.7 dynamic_slice.16
  42.7 1.9 %all-to-all-done.1 = bf16[2,1,1]{2,1,0:T(2,128)(2,1)S(1)} async-done(((bf16[2,1,1]{2,1,0:T(2,128)(2,1)}), bf16[2,1,1]{2,1,0:T(2,128)(2,1)S(1)}, u32[]{:S(2)}, u32[]{:S(2)}) %all-to-all-start.1) | async-done | bytes 36 | tf_op jit(solution)/shard_map/all_to_all | solution.py:29
  44.6 0.5 constant_dynamic-slice_fusion
  46.4 0.0 copy-done.2
  46.4 90.8 %all-reduce.2.cloned.1.call-done = f32[768,768]{1,0:T(8,128)} async-done(((f32[768,768]{1,0:T(8,128)}), f32[768,768]{1,0:T(8,128)}) %all-reduce.2.cloned.1.call-update) | async-done | bytes 2359312 | tf_op jit(solution)/shard_map/psum | solution.py:38
  137.2 3.0 %copy.7 = f32[768,768]{0,1:T(8,128)} copy(f32[768,768]{1,0:T(8,128)} %all-reduce.2.cloned.1.call-done) | data formatting | bytes 4718592 | tf_op jit(solution)/shard_map/psum | solution.py:38
  140.3 2.9 %fusion.1 = bf16[768,768]{0,1:T(8,128)(2,1)S(1)} fusion(f32[768,768]{1,0:T(8,128)} %all-reduce.2.cloned.1.call-done, f32[768,768]{0,1:T(8,128)} %copy.7, f32[768]{0:T(1024)S(1)} %copy-done.2, f32[768]{0:T(1024)S(1)} %broadcast_subtract_fusion), kind=kLoop, calls=%fused_computation.4 | loop fusion | flops 2949120 | bytes 5904384 | tf_op jit(solution)/shard_map/convert_element_type | solution.py:40
  143.1 0.8 fusion.3
  143.9 0.8 fusion.2
  144.7 1.3 pad_maximum_fusion
  (4 shorter events, 0.0 us)
Async XLA Ops:
  6.5 4.5 %copy-start = (bf16[2,512,768]{2,1,0:T(8,128)(2,1)S(1)}, bf16[2,512,768]{2,1,0:T(8,128)(2,1)}, u32[]{:S(2)}) copy-start(bf16[2,512,768]{2,1,0:T(8,128)(2,1)} %param.4) | copy-start | bytes 4718596
  13.1 3.9 %copy-start.3 = (s32[1,2]{1,0:T(1,128)S(1)}, s32[1,2]{1,0:T(1,128)}, u32[]{:S(2)}) copy-start(s32[1,2]{1,0:T(1,128)} %param.7) | copy-start | bytes 28
  13.1 21.6 %all-to-all-start = ((bf16[2,512,768]{2,1,0:T(8,128)(2,1)}), bf16[2,512,768]{2,1,0:T(8,128)(2,1)S(1)}, u32[]{:S(2)}, u32[]{:S(2)}) async-start(bf16[2,512,768]{2,1,0:T(8,128)(2,1)} %select_select_fusion), calls=%async_computation | async-start | bytes 3145728 | tf_op jit(solution)/shard_map/all_to_all | solution.py:28
  16.9 120.3 %all-reduce.2.cloned.1.call-start = ((), (), s32[]{:S(2)}) async-start(), calls=%async_computation.2 | async-start | bytes 4718592 | tf_op jit(solution)/shard_map/psum | solution.py:38
  36.8 0.7 copy-start.1
  36.8 9.6 %copy-start.2 = (f32[768]{0:T(1024)S(1)}, f32[768]{0:T(1024)}, u32[]{:S(2)}) copy-start(f32[768]{0:T(1024)} %param.6) | copy-start | bytes 9220
  38.8 5.7 %all-to-all-start.1 = ((bf16[2,1,1]{2,1,0:T(2,128)(2,1)}), bf16[2,1,1]{2,1,0:T(2,128)(2,1)S(1)}, u32[]{:S(2)}, u32[]{:S(2)}) async-start(bf16[2,1,1]{2,1,0:T(2,128)(2,1)} %copy.8), calls=%async_computation.1 | async-start | bytes 2048 | tf_op jit(solution)/shard_map/all_to_all | solution.py:29
Sparse Core Ops, SparseCore 0:
  37.0 100.1 all-reduce.1
where the time goes:
time: 155 us; the launch traced here: 153 us
  waiting for transfers between devices  107 us (69%)
  between operations  18 us (12%)
  local copies, waits for them, and re-layouts  7.59 us (5%)
  starting transfers between devices  7.04 us (5%)
  other arithmetic  5.87 us (4%)
  blocking collectives  3.96 us (3%)
  matrix products  3.8 us (2%)
    psum x1, waiting for transfers between devices, on_device(): integrals = lax.psum(partial_sum, 'aux')  90.8 us
    all_to_all x1, waiting for transfers between devices, on_device(): lax.all_to_all(owned_rows, 'occ', split_axis=0, concat_axis=0, tiled=True)  13.9 us
    all_gather x1, blocking collectives, on_device(): listed = lax.all_gather(pairs, 'occ', axis=0, tiled=True)  3.96 us
    all_to_all x1, starting transfers between devices, on_device(): lax.all_to_all(owned_rows, 'occ', split_axis=0, concat_axis=0, tiled=True)  3.8 us
    all_to_all x1, starting transfers between devices, on_device(): lax.all_to_all(owned_energy, 'occ', split_axis=0, concat_axis=0, tiled=True)  3.19 us
  transfers between devices with their start and end apart: 3, of which 3 were waited for; matrix products, arithmetic and copies ran while one was open for 2% of the time, Pallas kernels for 0%

commit v1 on v0

v1 whole, which is shorter than its diff:
```python
import functools

import jax
import jax.numpy as jnp
from jax import lax
from jax.experimental import pallas as pl
from jax.experimental.pallas import tpu as pltpu
from jax.sharding import PartitionSpec as P

LANES = 128
CORES = 2
ROWS_Y = 2
WIDTH = 256
MESH = pl.DeviceIdType.MESH
F32 = jnp.float32
BF16 = jnp.bfloat16


def plan_of(columns, layers):
    strips = columns // WIDTH
    chunks = [[s] for s in range(strips)]
    if any((s + 1) * WIDTH % (ROWS_Y * layers * 16) for s in range(strips)):
        chunks = [list(range(strips))]
    stages = ["X", "C", "Y", "Z", "AZ", "AY", "AC"]
    if len(chunks) == 3:
        order = [(0, "X"), (0, "C"), (0, "Y"), (1, "X"), (0, "Z"), (1, "C"), (0, "AZ")]
        order += [(1, "Y"), (2, "X"), (0, "AY"), (2, "C"), (1, "Z"), (0, "AC"), (2, "Y")]
        order += [(1, "AZ"), (2, "Z"), (1, "AY"), (2, "AZ"), (1, "AC"), (2, "AY"), (2, "AC")]
    else:
        order = [(k, s) for s in stages for k in range(len(chunks))]
    return chunks, order


def layout_of(chunk, layers):
    rows = sum((s + 1) * WIDTH for s in chunk)
    return rows, rows // (ROWS_Y * layers)


def body(groups, layers, pairs_ref, msg_ref, virt_ref, f_hbm, out_ref, *scratch):
    scratch = list(scratch)
    take = lambda: scratch.pop(0)
    slab, depth, columns = f_hbm.shape
    chunks, order = plan_of(columns, layers)
    f_ref, msgs, stage, bi, bj, acc = [take() for _ in range(6)]
    slots = [take() for _ in range(columns // WIDTH)]
    per_chunk = [[take() for _ in range(9)] for _ in chunks]
    (f_sem, m_send, m_recv, x_send, x_recv, c_sem, y_sem, z_send, z_recv, az_send, az_recv, ay_sem, ac_sem) = [
        take() for _ in range(13)
    ]

    aux = lax.axis_index("aux")
    occ = lax.axis_index("occ")
    core = lax.rem(aux, CORES)
    row = lax.rem(aux // CORES, ROWS_Y)
    layer = aux // (CORES * ROWS_Y)

    def device(z, y, c, g):
        return {"aux": (z * ROWS_Y + y) * CORES + c, "occ": g}

    core_peer = device(layer, row, 1 - core, occ)
    row_peer = device(layer, 1 - row, core, occ)
    layer_peer = lambda j: device(lax.rem(layer + j, layers), row, core, occ)
    occ_peer = lambda d: {"aux": aux, "occ": lax.rem(occ + groups - d, groups)}

    load = pltpu.make_async_copy(f_hbm, f_ref, f_sem)
    load.start()
    barrier = pltpu.get_barrier_semaphore()
    peers = [core_peer, row_peer]
    peers += [layer_peer(j) for j in range(1, layers)]
    peers += [occ_peer(d) for d in range(1, groups)]
    for peer in peers:
        pl.semaphore_signal(barrier, inc=1, device_id=peer, device_id_type=MESH)
    pl.semaphore_wait(barrier, len(peers))

    started = []

    def send(src, dst, send_sem, recv_sem, peer):
        copy = pltpu.make_async_remote_copy(
            src_ref=src, dst_ref=dst, send_sem=send_sem, recv_sem=recv_sem, device_id=peer, device_id_type=MESH
        )
        copy.start()
        started.append(copy)
        return copy

    def landed(ref, send_sem, recv_sem, peer):
        pltpu.make_async_remote_copy(
            src_ref=ref, dst_ref=ref, send_sem=send_sem, recv_sem=recv_sem, device_id=peer, device_id_type=MESH
        ).wait_recv()

    sent = [send(msg_ref, msgs.at[d], m_send.at[d], m_recv.at[d], occ_peer(d)) for d in range(1, groups)]
    msgs[0] = msg_ref[...]
    load.wait()
    i_local = lax.rem(pairs_ref[0, 0], slab)
    j_slab = pairs_ref[0, 1] // slab
    j_local = pairs_ref[0, 1] - j_slab * slab
    distance = lax.rem(j_slab - occ + groups, groups)
    for d in range(1, groups):
        sent[d - 1].wait_recv()
    strips = columns // WIDTH
    for s in range(strips):
        cols = slice(s * WIDTH, (s + 1) * WIDTH)
        for d in range(1, groups):
            asked = msgs[groups - d]
            rows = jnp.zeros((depth, WIDTH), BF16)
            for o in range(slab):
                mask = jnp.concatenate([asked[o : o + 1]] * (WIDTH // LANES), axis=1).astype(BF16)
                rows = rows + f_ref[o, :, cols] * mask
            stage[d - 1, s] = rows
            send(stage.at[d - 1, s], slots[s].at[d], x_send.at[d, s], x_recv.at[d, s], occ_peer(d))
    for s in range(strips):
        cols = slice(s * WIDTH, (s + 1) * WIDTH)
        slots[s][0] = f_ref[j_local, :, cols]
    bi[...] = f_ref[i_local]
    energy = msgs[0, pl.ds(slab + i_local, 1), :] + msgs[distance, pl.ds(slab + j_local, 1), :]

    down = []
    for t in range(columns // LANES):
        down.append(jnp.broadcast_to(virt_ref[t : t + 1, :], (LANES, LANES)).T)
    for k, chunk in enumerate(chunks):
        v_rows, v_lanes = per_chunk[k][7:9]
        base = 0
        for s in chunk:
            size = (s + 1) * WIDTH
            for t in range(size // LANES):
                v_rows[base + t * LANES : base + (t + 1) * LANES, :] = down[t]
            for c in range(CORES):
                index = s * (WIDTH // LANES) + c
                v_lanes[c, base : base + size, :] = jnp.broadcast_to(virt_ref[index : index + 1, :], (size, LANES))
            base += size

    def over_q(left, right):
        return lax.dot_general(left, right, (((0,), (0,)), ((), ())), preferred_element_type=F32)

    pending = {}

    def run_stage(k, name):
        chunk = chunks[k]
        part, give, got_c, give_y, got_y, give_z, amp, v_rows, v_lanes = per_chunk[k]
        rows, block = layout_of(chunk, layers)
        if name == "X":
            base = 0
            for s in chunk:
                end = (s + 1) * WIDTH
                cols = slice(s * WIDTH, end)
                for d in range(1, groups):
                    landed(slots[s].at[d], x_send.at[d, s], x_recv.at[d, s], occ_peer(d))
                bj[:, cols] = slots[s][distance]
                for w in range(2):
                    left, right = (bi, bj) if w == 0 else (bj, bi)
                    value = over_q(left[:, :end], right[:, cols])
                    for c in range(CORES):
                        part[c, w, base : base + end, :] = value[:, c * LANES : (c + 1) * LANES]
                base += end
            give[...] = part[1 - core].astype(BF16)
            pending[k, "C"] = send(give, got_c, c_sem.at[0, k], c_sem.at[1, k], core_peer)
        elif name == "C":
            pending[k, "C"].wait_recv()
            half = rows // ROWS_Y
            there = pl.ds(pl.multiple_of((1 - row) * half, half), half)
            here = pl.ds(pl.multiple_of(row * half, half), half)
            give_y[...] = (part[core, :, there, :] + got_c[:, there, :].astype(F32)).astype(BF16)
            pending[k, "Y"] = send(give_y, got_y, y_sem.at[0, k], y_sem.at[1, k], row_peer)
            part[0, :, 0:half, :] = part[core, :, here, :] + got_c[:, here, :].astype(F32)
        elif name == "Y":
            pending[k, "Y"].wait_recv()
            for j in range(1, layers):
                z = lax.rem(layer + j, layers)
                there = pl.ds(pl.multiple_of(z * block, block), block)
                give_z[0, j] = (part[0, :, there, :] + got_y[:, there, :].astype(F32)).astype(BF16)
                send(give_z.at[0, j], give_z.at[1, j], z_send.at[k, j], z_recv.at[k, j], layer_peer(j))
        elif name == "Z":
            here = pl.ds(pl.multiple_of(layer * block, block), block)
            total = part[0, :, here, :] + got_y[:, here, :].astype(F32)
            for j in range(1, layers):
                landed(give_z.at[1, j], z_send.at[k, j], z_recv.at[k, j], layer_peer(j))
                total = total + give_z[1, j].astype(F32)
            mine = pl.ds(pl.multiple_of((row * layers + layer) * block, block), block)
            down_rows = v_rows[mine, :]
            along = v_lanes[core, mine, :]
            first = (2.0 * total[0] - total[1]) / (energy - down_rows - along)
            second = (2.0 * total[1] - total[0]) / (energy - along - down_rows)
            amp[core, row, layer, 0] = first.astype(BF16)
            amp[core, row, layer, 1] = second.astype(BF16)
            home = amp.at[core, row, layer]
            for j in range(1, layers):
                send(home, home, az_send.at[k, j], az_recv.at[k, j], layer_peer(j))
        elif name == "AZ":
            for j in range(1, layers):
                z = lax.rem(layer + layers - j, layers)
                landed(amp.at[core, row, z], az_send.at[k, j], az_recv.at[k, j], layer_peer(j))
            home = amp.at[core, row]
            send(home, home, ay_sem.at[0, k], ay_sem.at[1, k], row_peer)
        elif name == "AY":
            landed(amp.at[core, 1 - row], ay_sem.at[0, k], ay_sem.at[1, k], row_peer)
            home = amp.at[core]
            send(home, home, ac_sem.at[0, k], ac_sem.at[1, k], core_peer)
        else:
            landed(amp.at[1 - core], ac_sem.at[0, k], ac_sem.at[1, k], core_peer)
            base = 0
            whole = []
            for w in range(2):
                halves = [amp[c, :, :, w].reshape(rows, LANES) for c in range(CORES)]
                whole.append(jnp.concatenate(halves, axis=1))
            for s in chunk:
                start, end = s * WIDTH, (s + 1) * WIDTH
                cols = slice(start, end)
                for w in range(2):
                    b = bj if w == 0 else bi
                    plain = whole[1 - w][base : base + end]
                    acc[w, :, cols] = jnp.dot(b[:, :end], plain, preferred_element_type=F32)
                    if start:
                        turned = whole[w][base : base + start]
                        acc[w, :, :start] += lax.dot_general(
                            b[:, cols], turned, (((1,), (1,)), ((), ())), preferred_element_type=F32
                        )
                base += end

    for k, name in order:
        run_stage(k, name)
    out_ref[...] = acc[...].astype(BF16)
    for copy in started:
        copy.wait_send()


def on_device(mesh_shape, factors, occ_energy, virt_energy, pairs):
    groups = mesh_shape["occ"]
    layers = mesh_shape["aux"] // (CORES * ROWS_Y)
    slab, depth, columns = factors.shape
    chunks, _ = plan_of(columns, layers)
    strips = columns // WIDTH
    asked = (jnp.arange(slab) == pairs[0, 1] % slab).astype(F32)
    msg = jnp.concatenate([asked, occ_energy.astype(F32)])
    msg = jnp.broadcast_to(msg[:, None], (2 * slab, LANES))
    scratch = [
        pltpu.VMEM((slab, depth, columns), BF16),
        pltpu.VMEM((groups, 2 * slab, LANES), F32),
        pltpu.VMEM((groups - 1, strips, depth, WIDTH), BF16),
        pltpu.VMEM((depth, columns), BF16),
        pltpu.VMEM((depth, columns), BF16),
        pltpu.VMEM((2, depth, columns), F32),
    ]
    scratch += [pltpu.VMEM((groups, depth, WIDTH), BF16)] * strips
    for chunk in chunks:
        rows, block = layout_of(chunk, layers)
        scratch += [
            pltpu.VMEM((CORES, 2, rows, LANES), F32),
            pltpu.VMEM((2, rows, LANES), BF16),
            pltpu.VMEM((2, rows, LANES), BF16),
            pltpu.VMEM((2, rows // ROWS_Y, LANES), BF16),
            pltpu.VMEM((2, rows // ROWS_Y, LANES), BF16),
            pltpu.VMEM((2, layers, 2, block, LANES), BF16),
            pltpu.VMEM((CORES, ROWS_Y, layers, 2, block, LANES), BF16),
            pltpu.VMEM((rows, LANES), F32),
            pltpu.VMEM((CORES, rows, LANES), F32),
        ]
    n = len(chunks)
    dma = pltpu.SemaphoreType.DMA
    scratch += [dma(())]
    scratch += [dma((groups,))] * 2
    scratch += [dma((groups, strips))] * 2
    scratch += [dma((2, n))] * 2
    scratch += [dma((n, layers))] * 4
    scratch += [dma((2, n))] * 2
    vmem = pl.BlockSpec(memory_space=pltpu.VMEM)
    out = pl.pallas_call(
        functools.partial(body, groups, layers),
        out_shape=jax.ShapeDtypeStruct((2, depth, columns), BF16),
        in_specs=[pl.BlockSpec(memory_space=pltpu.SMEM), vmem, vmem, pl.BlockSpec(memory_space=pl.ANY)],
        out_specs=vmem,
        scratch_shapes=scratch,
        compiler_params=pltpu.CompilerParams(
            collective_id=0, has_side_effects=True, vmem_limit_bytes=60 * 1024 * 1024
        ),
    )(pairs, msg, virt_energy.reshape(columns // LANES, LANES), factors)
    return out[None]


def solution(mesh):
    in_specs = (P("occ", "aux", None), P("occ"), P(), P("occ", None))
    out_specs = P("occ", None, "aux", None)
    return jax.shard_map(
        functools.partial(on_device, dict(mesh.shape)),
        mesh=mesh,
        in_specs=in_specs,
        out_specs=out_specs,
        check_vma=False,
    )
```

time: 155 us -> 63.8 us (0.41); the launches traced: 153 us -> 63.5 us
  waiting for transfers between devices: 107 us -> 0 us
  Pallas kernels: 0 us -> 56.3 us
  between operations: 18 us -> 1.97 us
  starting transfers between devices: 7.04 us -> 0 us
  other arithmetic: 5.87 us -> 0.74 us
  blocking collectives: 3.96 us -> 0 us
  matrix products: 3.8 us -> 0 us
  local copies, waits for them, and re-layouts: 7.59 us -> 4.54 us
    psum x1 -> x0, waiting for transfers between devices: 90.8 us -> none  [on_device(): integrals = lax.psum(partial_sum, 'aux')]
    pallas_call x0 -> x1, Pallas kernels: none -> 56.3 us  [on_device(): pl.pallas_call(functools.partial(body, groups, layers), out_shape=jax.Sha...]
    all_to_all x2 -> x0, waiting for transfers between devices: 15.8 us -> none  [the longest x1 13.9 us: on_device(): lax.all_to_all(owned_rows, 'occ', split_axis=0, concat_axis=0, tiled=True)]
    all_to_all x2 -> x0, starting transfers between devices: 7 us -> none  [the longest x1 3.8 us: on_device(): lax.all_to_all(owned_rows, 'occ', split_axis=0, concat_axis=0, tiled=True)]
    all_gather x1 -> x0, blocking collectives: 3.96 us -> none  [on_device(): listed = lax.all_gather(pairs, 'occ', axis=0, tiled=True)]
    dot_general x3 -> x0, matrix products: 3.8 us -> none  [the longest x1 2.22 us: on_device(): lax.dot_general(first_rows, second_rows, (((0,), (0,)), ((), ())), prefer...]
    psum x1 -> x0, local copies, waits for them, and re-layouts: 3.04 us -> none  [on_device(): integrals = lax.psum(partial_sum, 'aux')]
    convert_element_type x1 -> x2, other arithmetic: 2.85 us -> 0.66 us  [the longest x1 0.66 us: on_device(): msg = jnp.concatenate([asked, occ_energy.astype(F32)])]
  transfers between devices with their start and end apart: 3 -> 0, of which waited for: 3 -> 0; matrix products, arithmetic and copies ran while one was open for 2% -> 0% of each run, Pallas kernels for 0% -> 0%
where the time goes in v1:
time: 63.8 us; the launch traced here: 63.5 us
  Pallas kernels  56.3 us (88%)
  local copies, waits for them, and re-layouts  4.54 us (7%)
  between operations  1.97 us (3%)
  other arithmetic  0.74 us (1%)
    pallas_call x1, Pallas kernels, on_device(): pl.pallas_call(functools.partial(body, groups, layers), out_shape=jax.Sha...  56.3 us
    unnamed x1, local copies, waits for them, and re-layouts  2.65 us

profile of v1, /device:TPU:1, one launch (start us, length us, event | category | flops | bytes accessed | tf_op | source)
XLA Modules:
  0.0 63.5 jit_solution(10123375497641136767)
XLA Ops:
  0.0 1.2 %slice.3 = s32[1,1]{1,0:T(1,128)} slice(s32[1,2]{1,0:T(1,128)} %pairs_ref.1), slice={[0:1], [1:2]} | slice | bytes 8 | tf_op jit(solution)/shard_map/slice | solution.py:231
  3.2 0.7 %convert_element_type.7 = f32[2]{0:T(128)S(1)} convert(bf16[2]{0:T(256)(128)(2,1)} %param.5) | non-fusion elementwise | flops 2 | bytes 12 | tf_op jit(solution)/shard_map/convert_element_type | solution.py:232
  3.9 0.1 pad_maximum_fusion
  3.9 0.6 %broadcast_in_dim.4.msg_ref = f32[4,128]{1,0:T(4,128)} broadcast(f32[4]{0:T(128)S(1)} %pad_maximum_fusion), dimensions={0} | broadcast | bytes 2064 | tf_op jit(solution)/shard_map/broadcast_in_dim | solution.py:233
  4.6 56.3 %shard_map.46 = bf16[2,512,768]{2,1,0:T(8,128)(2,1)} custom-call(s32[1,2]{1,0:T(1,128)} %pairs_ref.1, f32[4,128]{1,0:T(4,128)} %broadcast_in_dim.4.msg_ref, f32[6,128]{1,0:T(8,128)} %bitcast.4, bf16[2,512,768]{2,1,0:T(8,128)(2,1)} %f_hbm.1), custom_call_target="tpu_custom_call" | custom-call | tf_op jit(solution)/shard_map/pallas_call | solution.py:265
  60.9 2.7 %copy.6 = bf16[1,2,512,768]{3,2,1,0:T(8,128)(2,1)} copy(bf16[1,2,512,768]{3,2,1,0:T(8,128)(2,1)} %bitcast.3) | data formatting | bytes 3145728
  (1 shorter events, 0.0 us)

commit v2 on v1

v2 whole, which is shorter than its diff:
```python
import functools

import jax
import jax.numpy as jnp
from jax import lax
from jax.experimental import pallas as pl
from jax.experimental.pallas import tpu as pltpu
from jax.sharding import PartitionSpec as P

LANES = 128
GRANT = 40 * 1024 * 1024
CORES = 2
ROWS_Y = 2
MESH = pl.DeviceIdType.MESH
F32 = jnp.float32
BF16 = jnp.bfloat16


def plan_of(columns, layers):
    strips = columns // LANES
    unit = CORES * ROWS_Y * layers * 16

    def fit(members):
        sizes = [(s + 1) * LANES for s in members]
        for at in reversed(range(len(members))):
            while sum(sizes) % unit and sizes[at] < columns:
                sizes[at] += LANES
        return [(s, (s + 1) * LANES, size) for s, size in zip(members, sizes)]

    split = [list(range(strips // 2))] + [[s] for s in range(strips // 2, strips)]
    chunks = [fit(members) for members in split]
    if any(sum(size for _, _, size in chunk) % unit for chunk in chunks):
        chunks = [fit(list(range(strips)))]
    stages = ["X", "C", "Y", "Z", "AZ", "AY", "AC"]
    when = {"X": 9, "C": 11, "Y": 15, "Z": 19, "AZ": 23, "AY": 27, "AC": 28}
    order = sorted((when[s] + 3 * k, k, stages.index(s), s) for s in stages for k in range(len(chunks)))
    return chunks, [(k, s) for _, k, _, s in order]


def layout_of(chunk, layers):
    rows = sum(size for _, _, size in chunk)
    return rows, rows // (CORES * ROWS_Y * layers)


def body(groups, layers, pairs_ref, energy_ref, virt_ref, f_hbm, out_ref, *scratch):
    scratch = list(scratch)
    take = lambda: scratch.pop(0)
    slab, depth, columns = f_hbm.shape
    chunks, order = plan_of(columns, layers)
    f_ref, msgs, bi, bj, bi_t, bj_t, acc = [take() for _ in range(7)]
    per_chunk = [[take() for _ in range(11)] for _ in chunks]
    (f_sem, m_send, m_recv, x_send, x_recv, c_sem, y_sem, z_send, z_recv, az_send, az_recv, ay_sem, ac_sem) = [
        take() for _ in range(13)
    ]

    aux = lax.axis_index("aux")
    occ = lax.axis_index("occ")
    core = lax.rem(aux, CORES)
    row = lax.rem(aux // CORES, ROWS_Y)
    layer = aux // (CORES * ROWS_Y)

    def device(z, y, c, g):
        return {"aux": (z * ROWS_Y + y) * CORES + c, "occ": g}

    core_peer = device(layer, row, 1 - core, occ)
    row_peer = device(layer, 1 - row, core, occ)
    layer_peer = lambda j: device(lax.rem(layer + j, layers), row, core, occ)
    occ_peer = lambda d: {"aux": aux, "occ": lax.rem(occ + groups - d, groups)}

    load = pltpu.make_async_copy(f_hbm, f_ref, f_sem)
    load.start()
    barrier = pltpu.get_barrier_semaphore()
    peers = [core_peer, row_peer]
    peers += [layer_peer(j) for j in range(1, layers)]
    peers += [occ_peer(d) for d in range(1, groups)]
    for peer in peers:
        pl.semaphore_signal(barrier, inc=1, device_id=peer, device_id_type=MESH)
    pl.semaphore_wait(barrier, len(peers))

    started = []

    def send(src, dst, send_sem, recv_sem, peer):
        copy = pltpu.make_async_remote_copy(
            src_ref=src, dst_ref=dst, send_sem=send_sem, recv_sem=recv_sem, device_id=peer, device_id_type=MESH
        )
        copy.start()
        started.append(copy)
        return copy

    def landed(ref, send_sem, recv_sem, peer):
        pltpu.make_async_remote_copy(
            src_ref=ref, dst_ref=ref, send_sem=send_sem, recv_sem=recv_sem, device_id=peer, device_id_type=MESH
        ).wait_recv()

    i_local = lax.rem(pairs_ref[0, 0], slab)
    j_slab = pairs_ref[0, 1] // slab
    j_local = pairs_ref[0, 1] - j_slab * slab
    distance = lax.rem(j_slab - occ + groups, groups)
    slab_energy = energy_ref[...].astype(F32)
    for o in range(slab):
        wants = jnp.where(j_local == o, 1.0, 0.0).astype(F32)
        msgs[0, o : o + 1, :] = jnp.full((1, LANES), wants, F32)
        msgs[0, slab + o : slab + o + 1, :] = jnp.broadcast_to(slab_energy[:, o : o + 1], (1, LANES))
    sent = [send(msgs.at[0], msgs.at[d], m_send.at[d], m_recv.at[d], occ_peer(d)) for d in range(1, groups)]
    load.wait()
    for d in range(1, groups):
        sent[d - 1].wait_recv()

    def columns_of(chunk):
        return slice(chunk[0][0] * LANES, chunk[-1][1])

    for k, chunk in enumerate(chunks):
        cols = columns_of(chunk)
        stage, slots = per_chunk[k][9:11]
        for d in range(1, groups):
            asked = msgs[groups - d]
            rows = jnp.zeros((depth, cols.stop - cols.start), BF16)
            for o in range(slab):
                mask = jnp.concatenate([asked[o : o + 1]] * len(chunk), axis=1).astype(BF16)
                rows = rows + f_ref[o, :, cols] * mask
            stage[d - 1] = rows
            send(stage.at[d - 1], slots.at[d], x_send.at[d, k], x_recv.at[d, k], occ_peer(d))
    for k, chunk in enumerate(chunks):
        per_chunk[k][10][0] = f_ref[j_local, :, columns_of(chunk)]
    bi[...] = f_ref[i_local]
    bi_t[...] = bi[...].T
    energy = msgs[0, pl.ds(slab + i_local, 1), :] + msgs[distance, pl.ds(slab + j_local, 1), :]

    down = []
    for t in range(columns // LANES):
        down.append(jnp.broadcast_to(virt_ref[t : t + 1, :], (LANES, LANES)).T)
    for k, chunk in enumerate(chunks):
        part, v_rows, v_lanes = per_chunk[k][0], *per_chunk[k][7:9]
        base = 0
        for s, end, size in chunk:
            for t in range(size // LANES):
                v_rows[base + t * LANES : base + (t + 1) * LANES, :] = down[t]
            v_lanes[base : base + size, :] = jnp.broadcast_to(virt_ref[s : s + 1, :], (size, LANES))
            if size > end:
                part[:, base + end : base + size, :] = jnp.zeros((2, size - end, LANES), F32)
            base += size

    pending = {}

    def run_stage(k, name):
        chunk = chunks[k]
        part, give, got_c, give_y, got_y, give_z, amp, v_rows, v_lanes, stage, slots = per_chunk[k]
        rows, block = layout_of(chunk, layers)
        half, quarter = rows // CORES, rows // (CORES * ROWS_Y)

        def span(index, size):
            return pl.ds(pl.multiple_of(index * size, size), size)

        if name == "X":
            for d in range(1, groups):
                landed(slots.at[d], x_send.at[d, k], x_recv.at[d, k], occ_peer(d))
            cols = columns_of(chunk)
            arrived = slots[distance]
            bj[:, cols] = arrived
            bj_t[cols, :] = arrived.T
            base = 0
            for s, end, size in chunk:
                cols = slice(s * LANES, end)
                part[0, base : base + end, :] = jnp.dot(bi_t[:end, :], bj[:, cols], preferred_element_type=F32)
                part[1, base : base + end, :] = jnp.dot(bj_t[:end, :], bi[:, cols], preferred_element_type=F32)
                base += size
            give[...] = part[:, span(1 - core, half), :].astype(BF16)
            pending[k, "C"] = send(give, got_c, c_sem.at[0, k], c_sem.at[1, k], core_peer)
        elif name == "C":
            pending[k, "C"].wait_recv()
            there = span(core * ROWS_Y + 1 - row, quarter)
            here = span(core * ROWS_Y + row, quarter)
            give_y[...] = (part[:, there, :] + got_c[:, span(1 - row, quarter), :].astype(F32)).astype(BF16)
            pending[k, "Y"] = send(give_y, got_y, y_sem.at[0, k], y_sem.at[1, k], row_peer)
            part[:, here, :] = part[:, here, :] + got_c[:, span(row, quarter), :].astype(F32)
        elif name == "Y":
            pending[k, "Y"].wait_recv()
            base = (core * ROWS_Y + row) * layers
            for j in range(1, layers):
                z = lax.rem(layer + j, layers)
                give_z[0, j] = (part[:, span(base + z, block), :] + got_y[:, span(z, block), :].astype(F32)).astype(BF16)
                send(give_z.at[0, j], give_z.at[1, j], z_send.at[k, j], z_recv.at[k, j], layer_peer(j))
        elif name == "Z":
            mine = span((core * ROWS_Y + row) * layers + layer, block)
            total = part[:, mine, :] + got_y[:, span(layer, block), :].astype(F32)
            down_rows = v_rows[mine, :]
            along = v_lanes[mine, :]
            for j in range(1, layers):
                landed(give_z.at[1, j], z_send.at[k, j], z_recv.at[k, j], layer_peer(j))
                total = total + give_z[1, j].astype(F32)
            first = (2.0 * total[0] - total[1]) / (energy - down_rows - along)
            second = (2.0 * total[1] - total[0]) / (energy - along - down_rows)
            amp[core, row, layer, 0] = first.astype(BF16)
            amp[core, row, layer, 1] = second.astype(BF16)
            home = amp.at[core, row, layer]
            for j in range(1, layers):
                send(home, home, az_send.at[k, j], az_recv.at[k, j], layer_peer(j))
        elif name == "AZ":
            for j in range(1, layers):
                z = lax.rem(layer + layers - j, layers)
                landed(amp.at[core, row, z], az_send.at[k, j], az_recv.at[k, j], layer_peer(j))
            home = amp.at[core, row]
            send(home, home, ay_sem.at[0, k], ay_sem.at[1, k], row_peer)
        elif name == "AY":
            landed(amp.at[core, 1 - row], ay_sem.at[0, k], ay_sem.at[1, k], row_peer)
            home = amp.at[core]
            send(home, home, ac_sem.at[0, k], ac_sem.at[1, k], core_peer)
        else:
            landed(amp.at[1 - core], ac_sem.at[0, k], ac_sem.at[1, k], core_peer)
            whole = [amp[:, :, :, w].reshape(rows, LANES) for w in range(2)]
            base = 0
            for s, end, size in chunk:
                start = s * LANES
                cols = slice(start, end)
                last = end == columns
                for w in range(2):
                    b = bj if w == 0 else bi
                    plain = jnp.dot(b[:, :end], whole[1 - w][base : base + end], preferred_element_type=F32)
                    if last:
                        out_ref[w, :, cols] = plain.astype(BF16)
                    else:
                        acc[w, :, cols] = plain
                    if start:
                        turned = lax.dot_general(
                            b[:, cols],
                            whole[w][base : base + start],
                            (((1,), (1,)), ((), ())),
                            preferred_element_type=F32,
                        )
                        if last:
                            out_ref[w, :, :start] = (acc[w, :, :start] + turned).astype(BF16)
                        else:
                            acc[w, :, :start] += turned
                base += size

    for k, name in order:
        run_stage(k, name)
    for copy in started:
        copy.wait_send()


def on_device(mesh_shape, factors, occ_energy, virt_energy, pairs):
    groups = mesh_shape["occ"]
    layers = mesh_shape["aux"] // (CORES * ROWS_Y)
    slab, depth, columns = factors.shape
    chunks, _ = plan_of(columns, layers)
    scratch = [
        pltpu.VMEM((slab, depth, columns), BF16),
        pltpu.VMEM((groups, 2 * slab, LANES), F32),
        pltpu.VMEM((depth, columns), BF16),
        pltpu.VMEM((depth, columns), BF16),
        pltpu.VMEM((columns, depth), BF16),
        pltpu.VMEM((columns, depth), BF16),
        pltpu.VMEM((2, depth, columns), F32),
    ]
    for chunk in chunks:
        rows, block = layout_of(chunk, layers)
        width = len(chunk) * LANES
        scratch += [
            pltpu.VMEM((2, rows, LANES), F32),
            pltpu.VMEM((2, rows // CORES, LANES), BF16),
            pltpu.VMEM((2, rows // CORES, LANES), BF16),
            pltpu.VMEM((2, rows // (CORES * ROWS_Y), LANES), BF16),
            pltpu.VMEM((2, rows // (CORES * ROWS_Y), LANES), BF16),
            pltpu.VMEM((2, layers, 2, block, LANES), BF16),
            pltpu.VMEM((CORES, ROWS_Y, layers, 2, block, LANES), BF16),
            pltpu.VMEM((rows, LANES), F32),
            pltpu.VMEM((rows, LANES), F32),
            pltpu.VMEM((groups - 1, depth, width), BF16),
            pltpu.VMEM((groups, depth, width), BF16),
        ]
    n = len(chunks)
    dma = pltpu.SemaphoreType.DMA
    scratch += [dma(())]
    scratch += [dma((groups,))] * 2
    scratch += [dma((groups, n))] * 2
    scratch += [dma((2, n))] * 2
    scratch += [dma((n, layers))] * 4
    scratch += [dma((2, n))] * 2
    vmem = pl.BlockSpec(memory_space=pltpu.VMEM)
    out = pl.pallas_call(
        functools.partial(body, groups, layers),
        out_shape=jax.ShapeDtypeStruct((2, depth, columns), BF16),
        in_specs=[pl.BlockSpec(memory_space=pltpu.SMEM), vmem, vmem, pl.BlockSpec(memory_space=pl.ANY)],
        out_specs=vmem,
        scratch_shapes=scratch,
        compiler_params=pltpu.CompilerParams(
            collective_id=0, has_side_effects=True, vmem_limit_bytes=GRANT
        ),
    )(pairs, occ_energy[None], virt_energy.reshape(columns // LANES, LANES), factors)
    return out[None]


def solution(mesh):
    in_specs = (P("occ", "aux", None), P("occ"), P(), P("occ", None))
    out_specs = P("occ", None, "aux", None)
    return jax.shard_map(
        functools.partial(on_device, dict(mesh.shape)),
        mesh=mesh,
        in_specs=in_specs,
        out_specs=out_specs,
        check_vma=False,
    )
```

time: 63.8 us -> 55.6 us (0.87)
  Pallas kernels: 56.3 us -> 50.8 us
  between operations: 1.97 us -> 0.01 us
  other arithmetic: 0.74 us -> 0 us
    pallas_call x1, Pallas kernels: 56.3 us -> 50.8 us  [on_device(): pl.pallas_call(functools.partial(body, groups, layers), out_shape=jax.Sha...]
    unnamed x1 -> x9, local copies, waits for them, and re-layouts: 2.65 us -> 4.55 us
    slice x1 -> x0, local copies, waits for them, and re-layouts: 1.24 us -> none  [on_device(): asked = (jnp.arange(slab) == pairs[0, 1] % slab).astype(F32)]
    convert_element_type x2 -> x0, other arithmetic: 0.66 us -> none  [the longest x1 0.66 us: on_device(): msg = jnp.concatenate([asked, occ_energy.astype(F32)])]
    broadcast_in_dim x1 -> x0, local copies, waits for them, and re-layouts: 0.65 us -> none  [on_device(): msg = jnp.broadcast_to(msg[:, None], (2 * slab, LANES))]
where the time goes in v2:
time: 55.6 us; the launch traced here: 55.4 us
  Pallas kernels  50.8 us (91%)
  local copies, waits for them, and re-layouts  4.55 us (8%)
    pallas_call x1, Pallas kernels, on_device(): pl.pallas_call(functools.partial(body, groups, layers), out_shape=jax.Sha...  50.8 us
    unnamed x9, local copies, waits for them, and re-layouts  4.55 us

profile of v2, /device:TPU:1, one launch (start us, length us, event | category | flops | bytes accessed | tf_op | source)
XLA Modules:
  0.0 55.4 jit_solution(13673064361566798680)
XLA Ops:
  0.0 0.0 copy-start
  0.0 1.4 %copy-done = bf16[2,512,768]{2,1,0:T(8,128)(2,1)S(1)} copy-done((bf16[2,512,768]{2,1,0:T(8,128)(2,1)S(1)}, bf16[2,512,768]{2,1,0:T(8,128)(2,1)}, u32[]{:S(2)}) %copy-start) | copy-done | bytes 1572888
  1.4 0.0 copy-start.1
  1.4 0.7 %copy-done.1 = f32[768]{0:T(1024)S(1)} copy-done((f32[768]{0:T(1024)S(1)}, f32[768]{0:T(1024)}, u32[]{:S(2)}) %copy-start.1) | copy-done | bytes 3096
  2.1 0.0 copy-start.2
  2.1 0.7 %copy-done.2 = s32[1,2]{1,0:T(1,128)S(1)} copy-done((s32[1,2]{1,0:T(1,128)S(1)}, s32[1,2]{1,0:T(1,128)}, u32[]{:S(2)}) %copy-start.2) | copy-done | bytes 32
  2.8 0.0 copy-start.3
  2.8 0.7 %copy-done.3 = bf16[2]{0:T(256)(128)(2,1)S(1)} copy-done((bf16[2]{0:T(256)(128)(2,1)S(1)}, bf16[2]{0:T(256)(128)(2,1)}, u32[]{:S(2)}) %copy-start.3) | copy-done | bytes 28
  3.4 50.8 %shard_map.46 = bf16[2,512,768]{2,1,0:T(8,128)(2,1)S(1)} custom-call(s32[1,2]{1,0:T(1,128)S(1)} %copy-done.2, bf16[1,2]{1,0:T(2,128)(2,1)S(1)} %bitcast.5, f32[6,128]{1,0:T(8,128)S(1)} %bitcast.4, bf16[2,512,768]{2,1,0:T(8,128)(2,1)S(1)} %copy-done), custom_call_target="tpu_custom_call" | custom-call | tf_op jit(solution)/shard_map/pallas_call | solution.py:281
  54.2 1.1 %copy.6 = bf16[1,2,512,768]{3,2,1,0:T(8,128)(2,1)} copy(bf16[1,2,512,768]{3,2,1,0:T(8,128)(2,1)S(1)} %bitcast.3) | data formatting | bytes 3145728
Async XLA Ops:
  0.0 1.4 %copy-start = (bf16[2,512,768]{2,1,0:T(8,128)(2,1)S(1)}, bf16[2,512,768]{2,1,0:T(8,128)(2,1)}, u32[]{:S(2)}) copy-start(bf16[2,512,768]{2,1,0:T(8,128)(2,1)} %f_hbm.1) | copy-start | bytes 4718596
  1.4 0.7 %copy-start.1 = (f32[768]{0:T(1024)S(1)}, f32[768]{0:T(1024)}, u32[]{:S(2)}) copy-start(f32[768]{0:T(1024)} %param.6) | copy-start | bytes 9220
  2.1 0.7 %copy-start.2 = (s32[1,2]{1,0:T(1,128)S(1)}, s32[1,2]{1,0:T(1,128)}, u32[]{:S(2)}) copy-start(s32[1,2]{1,0:T(1,128)} %pairs_ref.1) | copy-start | bytes 28
  2.8 0.7 %copy-start.3 = (bf16[2]{0:T(256)(128)(2,1)S(1)}, bf16[2]{0:T(256)(128)(2,1)}, u32[]{:S(2)}) copy-start(bf16[2]{0:T(256)(128)(2,1)} %param.5) | copy-start | bytes 16

commit v3 on v2

--- a/solution.py
+++ b/solution.py
@@ -42,11 +42,12 @@
     return rows, rows // (CORES * ROWS_Y * layers)
 
 
-def body(groups, layers, pairs_ref, energy_ref, virt_ref, f_hbm, out_ref, *scratch):
+def body(groups, layers, pairs_hbm, energy_hbm, virt_hbm, f_hbm, out_ref, *scratch):
     scratch = list(scratch)
     take = lambda: scratch.pop(0)
     slab, depth, columns = f_hbm.shape
     chunks, order = plan_of(columns, layers)
+    pairs_ref, energy_ref, virt_ref, small_sem = [take() for _ in range(4)]
     f_ref, msgs, bi, bj, bi_t, bj_t, acc = [take() for _ in range(7)]
     per_chunk = [[take() for _ in range(11)] for _ in chunks]
     (f_sem, m_send, m_recv, x_send, x_recv, c_sem, y_sem, z_send, z_recv, az_send, az_recv, ay_sem, ac_sem) = [
@@ -67,8 +68,18 @@
     layer_peer = lambda j: device(lax.rem(layer + j, layers), row, core, occ)
     occ_peer = lambda d: {"aux": aux, "occ": lax.rem(occ + groups - d, groups)}
 
-    load = pltpu.make_async_copy(f_hbm, f_ref, f_sem)
-    load.start()
+    def columns_of(chunk):
+        return slice(chunk[0][0] * LANES, chunk[-1][1])
+
+    small = []
+    for at, (src, dst) in enumerate([(pairs_hbm, pairs_ref), (energy_hbm, energy_ref), (virt_hbm, virt_ref)]):
+        small.append(pltpu.make_async_copy(src, dst, small_sem.at[at]))
+        small[at].start()
+    loads = []
+    for k, chunk in enumerate(chunks):
+        cols = columns_of(chunk)
+        loads.append(pltpu.make_async_copy(f_hbm.at[:, :, cols], f_ref.at[:, :, cols], f_sem.at[k]))
+        loads[k].start()
     barrier = pltpu.get_barrier_semaphore()
     peers = [core_peer, row_peer]
     peers += [layer_peer(j) for j in range(1, layers)]
@@ -92,6 +103,8 @@
             src_ref=ref, dst_ref=ref, send_sem=send_sem, recv_sem=recv_sem, device_id=peer, device_id_type=MESH
         ).wait_recv()
 
+    for copy in small:
+        copy.wait()
     i_local = lax.rem(pairs_ref[0, 0], slab)
     j_slab = pairs_ref[0, 1] // slab
     j_local = pairs_ref[0, 1] - j_slab * slab
@@ -102,14 +115,11 @@
         msgs[0, o : o + 1, :] = jnp.full((1, LANES), wants, F32)
         msgs[0, slab + o : slab + o + 1, :] = jnp.broadcast_to(slab_energy[:, o : o + 1], (1, LANES))
     sent = [send(msgs.at[0], msgs.at[d], m_send.at[d], m_recv.at[d], occ_peer(d)) for d in range(1, groups)]
-    load.wait()
     for d in range(1, groups):
         sent[d - 1].wait_recv()
 
-    def columns_of(chunk):
-        return slice(chunk[0][0] * LANES, chunk[-1][1])
-
     for k, chunk in enumerate(chunks):
+        loads[k].wait()
         cols = columns_of(chunk)
         stage, slots = per_chunk[k][9:11]
         for d in range(1, groups):
@@ -245,6 +255,10 @@
     slab, depth, columns = factors.shape
     chunks, _ = plan_of(columns, layers)
     scratch = [
+        pltpu.SMEM(pairs.shape, jnp.int32),
+        pltpu.VMEM((1, slab), BF16),
+        pltpu.VMEM((columns // LANES, LANES), F32),
+        pltpu.SemaphoreType.DMA((3,)),
         pltpu.VMEM((slab, depth, columns), BF16),
         pltpu.VMEM((groups, 2 * slab, LANES), F32),
         pltpu.VMEM((depth, columns), BF16),
@@ -271,23 +285,24 @@
         ]
     n = len(chunks)
     dma = pltpu.SemaphoreType.DMA
-    scratch += [dma(())]
+    scratch += [dma((n,))]
     scratch += [dma((groups,))] * 2
     scratch += [dma((groups, n))] * 2
     scratch += [dma((2, n))] * 2
     scratch += [dma((n, layers))] * 4
     scratch += [dma((2, n))] * 2
     vmem = pl.BlockSpec(memory_space=pltpu.VMEM)
+    operands = (pairs, occ_energy[None], virt_energy.reshape(columns // LANES, LANES), factors)
     out = pl.pallas_call(
         functools.partial(body, groups, layers),
         out_shape=jax.ShapeDtypeStruct((2, depth, columns), BF16),
-        in_specs=[pl.BlockSpec(memory_space=pltpu.SMEM), vmem, vmem, pl.BlockSpec(memory_space=pl.ANY)],
+        in_specs=[pl.BlockSpec(memory_space=pltpu.HBM)] * 4,
         out_specs=vmem,
         scratch_shapes=scratch,
         compiler_params=pltpu.CompilerParams(
             collective_id=0, has_side_effects=True, vmem_limit_bytes=GRANT
         ),
-    )(pairs, occ_energy[None], virt_energy.reshape(columns // LANES, LANES), factors)
+    )(*[pltpu.with_memory_space_constraint(x, pltpu.HBM) for x in operands])
     return out[None]
 
 

time: 55.6 us -> 51.4 us (0.924)
  local copies, waits for them, and re-layouts: 4.55 us -> 1.15 us
  Pallas kernels: 50.8 us -> 50.1 us
    unnamed x9 -> x1, local copies, waits for them, and re-layouts: 4.55 us -> 1.15 us
    pallas_call x1, Pallas kernels: 50.8 us -> 50.1 us  [on_device(): pl.pallas_call(functools.partial(body, groups, layers), out_shape=jax.Sha...]
where the time goes in v3:
time: 51.4 us; the launch traced here: 51.3 us
  Pallas kernels  50.1 us (97%)
  local copies, waits for them, and re-layouts  1.15 us (2%)
    pallas_call x1, Pallas kernels, on_device(): pl.pallas_call(functools.partial(body, groups, layers), out_shape=jax.Sha...  50.1 us
    unnamed x1, local copies, waits for them, and re-layouts  1.15 us

profile of v3, /device:TPU:1, one launch (start us, length us, event | category | flops | bytes accessed | tf_op | source)
XLA Modules:
  0.0 51.3 jit_solution(15908320987760830294)
XLA Ops:
  0.0 50.1 %shard_map.46 = bf16[2,512,768]{2,1,0:T(8,128)(2,1)S(1)} custom-call(s32[1,2]{1,0:T(1,128)} %pairs_hbm.1, bf16[1,2]{1,0:T(2,128)(2,1)} %bitcast.5, f32[6,128]{1,0:T(8,128)} %bitcast.4, bf16[2,512,768]{2,1,0:T(8,128)(2,1)} %f_hbm.1), custom_call_target="tpu_custom_call" | custom-call | tf_op jit(solution)/shard_map/pallas_call | solution.py:296
  50.2 1.1 %copy.6 = bf16[1,2,512,768]{3,2,1,0:T(8,128)(2,1)} copy(bf16[1,2,512,768]{3,2,1,0:T(8,128)(2,1)S(1)} %bitcast.3) | data formatting | bytes 3145728

commit v4 on v3

--- a/solution.py
+++ b/solution.py
@@ -50,8 +50,8 @@
     pairs_ref, energy_ref, virt_ref, small_sem = [take() for _ in range(4)]
     f_ref, msgs, bi, bj, bi_t, bj_t, acc = [take() for _ in range(7)]
     per_chunk = [[take() for _ in range(11)] for _ in chunks]
-    (f_sem, m_send, m_recv, x_send, x_recv, c_sem, y_sem, z_send, z_recv, az_send, az_recv, ay_sem, ac_sem) = [
-        take() for _ in range(13)
+    (f_sem, m_send, m_recv, x_send, x_recv, c_sem, y_sem, z_send, z_recv, az_send, az_recv, ay_send, ay_recv, ac_sem) = [
+        take() for _ in range(14)
     ]
 
     aux = lax.axis_index("aux")
@@ -205,18 +205,24 @@
             home = amp.at[core, row, layer]
             for j in range(1, layers):
                 send(home, home, az_send.at[k, j], az_recv.at[k, j], layer_peer(j))
+            send(home, home, ay_send.at[k, 0], ay_recv.at[k, 0], row_peer)
         elif name == "AZ":
             for j in range(1, layers):
                 z = lax.rem(layer + layers - j, layers)
-                landed(amp.at[core, row, z], az_send.at[k, j], az_recv.at[k, j], layer_peer(j))
+                block_ref = amp.at[core, row, z]
+                landed(block_ref, az_send.at[k, j], az_recv.at[k, j], layer_peer(j))
+                send(block_ref, block_ref, ay_send.at[k, j], ay_recv.at[k, j], row_peer)
             home = amp.at[core, row]
-            send(home, home, ay_sem.at[0, k], ay_sem.at[1, k], row_peer)
+            send(home, home, ac_sem.at[0, k, 0], ac_sem.at[1, k, 0], core_peer)
         elif name == "AY":
-            landed(amp.at[core, 1 - row], ay_sem.at[0, k], ay_sem.at[1, k], row_peer)
-            home = amp.at[core]
-            send(home, home, ac_sem.at[0, k], ac_sem.at[1, k], core_peer)
+            for j in range(layers):
+                z = lax.rem(layer + layers - j, layers)
+                landed(amp.at[core, 1 - row, z], ay_send.at[k, j], ay_recv.at[k, j], row_peer)
+            home = amp.at[core, 1 - row]
+            send(home, home, ac_sem.at[0, k, 1], ac_sem.at[1, k, 1], core_peer)
         else:
-            landed(amp.at[1 - core], ac_sem.at[0, k], ac_sem.at[1, k], core_peer)
+            landed(amp.at[1 - core, row], ac_sem.at[0, k, 0], ac_sem.at[1, k, 0], core_peer)
+            landed(amp.at[1 - core, 1 - row], ac_sem.at[0, k, 1], ac_sem.at[1, k, 1], core_peer)
             whole = [amp[:, :, :, w].reshape(rows, LANES) for w in range(2)]
             base = 0
             for s, end, size in chunk:
@@ -289,8 +295,8 @@
     scratch += [dma((groups,))] * 2
     scratch += [dma((groups, n))] * 2
     scratch += [dma((2, n))] * 2
-    scratch += [dma((n, layers))] * 4
-    scratch += [dma((2, n))] * 2
+    scratch += [dma((n, layers))] * 6
+    scratch += [dma((2, n, 2))]
     vmem = pl.BlockSpec(memory_space=pltpu.VMEM)
     operands = (pairs, occ_energy[None], virt_energy.reshape(columns // LANES, LANES), factors)
     out = pl.pallas_call(

time: 51.4 us -> 51 us (level)
  no operation moved by 1% of the time
where the time goes in v4:
time: 51 us; the launch traced here: 50.9 us
  Pallas kernels  49.8 us (98%)
  local copies, waits for them, and re-layouts  1.15 us (2%)
    pallas_call x1, Pallas kernels, on_device(): pl.pallas_call(functools.partial(body, groups, layers), out_shape=jax.Sha...  49.8 us
    unnamed x1, local copies, waits for them, and re-layouts  1.15 us

profile of v4, /device:TPU:1, one launch (start us, length us, event | category | flops | bytes accessed | tf_op | source)
XLA Modules:
  0.0 50.9 jit_solution(4005455843464017322)
XLA Ops:
  0.0 49.8 %shard_map.46 = bf16[2,512,768]{2,1,0:T(8,128)(2,1)S(1)} custom-call(s32[1,2]{1,0:T(1,128)} %pairs_hbm.1, bf16[1,2]{1,0:T(2,128)(2,1)} %bitcast.5, f32[6,128]{1,0:T(8,128)} %bitcast.4, bf16[2,512,768]{2,1,0:T(8,128)(2,1)} %f_hbm.1), custom_call_target="tpu_custom_call" | custom-call | tf_op jit(solution)/shard_map/pallas_call | solution.py:302
  49.8 1.1 %copy.6 = bf16[1,2,512,768]{3,2,1,0:T(8,128)(2,1)} copy(bf16[1,2,512,768]{3,2,1,0:T(8,128)(2,1)S(1)} %bitcast.3) | data formatting | bytes 3145728
